TPU v7x, 32 devices: a whole 2x2x4 slice. The times are simulated.
32 devices in a mesh: groups: 2 (over x), wide: 16 (over z, y, core).
Axes of the slice: x: 2, y: 2, z: 4, core: 2. Of those that a mesh axis runs over, the one named last changes fastest.
Arguments:
- prefix_hidden: bfloat16 [32, 256, 8192], P(('groups', 'wide')), parts along dimension 0, may hold values from -6 to 6
- prefix_lengths: int32 [32], P(('groups', 'wide')), parts along dimension 0, may hold values from 64 to 256
- action_noise: float32 [32, 50, 32], P(('groups', 'wide')), parts along dimension 0, may hold values from -4 to 4
- prefix_gain: float32 [8192], replicated, may hold values from 0.1 to 1.9
- key_weight: bfloat16 [8192, 512], P('wide'), may hold values from -0.0625 to 0.0625
- value_weight: bfloat16 [8192, 512], P('wide'), may hold values from -0.0625 to 0.0625
- input_weight: float32 [32, 1024], replicated, may hold values from -1 to 1
- expert_gain: float32 [1024], replicated, may hold values from 0.1 to 1.9
- expert_query: bfloat16 [1024, 1024], P('wide'), may hold values from -0.1875 to 0.1875
- expert_key: bfloat16 [1024, 512], P('wide'), may hold values from -5.3125 to 5.3125
- expert_value: bfloat16 [1024, 512], P('wide'), may hold values from -0.1875 to 0.1875
- expert_output: bfloat16 [1024, 1024], P('wide'), may hold values from -0.1875 to 0.1875
- final_gain: float32 [1024], replicated, may hold values from 0.1 to 1.9
- output_weight: bfloat16 [1024, 32], replicated, may hold values from -0.1875 to 0.1875
Outputs:
- actions: float32 [32, 50, 32], P(('groups', 'wide')), parts along dimension 0
There are 2 independent parts, one for each index of `groups`. A program takes and returns all parts, laid end to end along the dimension named above; an argument that names none is the same for every part. Nothing has to cross between parts.
Inputs may be any that keep to these rules, and one draw needn't show every extreme that they name: `prefix_lengths`: positions at or after a sample's length are padding and take no part.
All inputs are finite; a program needn't handle non-finite values.
Results may differ from a plain program's by a relative error of at most 0.0075.
Values may be sent and summed in bfloat16 or wider, within the bound.
A program may use at most 128 MiB of HBM per device.

v0:
```python
import jax
import jax.numpy as jnp
from jax import lax
from jax.sharding import PartitionSpec as P

HEAD = 128
STEPS = 4
rope_base = 1000000.0
norm_eps = 1e-06


def normalize(values, norm_gain):
    mean_square = jnp.mean(values * values, axis=-1, keepdims=True)
    return values * lax.rsqrt(mean_square + norm_eps) * norm_gain


def rotate(values, positions):
    half_width = values.shape[-1] // 2
    inv_freqs = rope_base ** (-jnp.arange(half_width, dtype=jnp.float32) * 2.0 / values.shape[-1])
    angles = positions[:, None] * inv_freqs[None, :]
    cosine = jnp.cos(angles)[:, None, :]
    sine_part = jnp.sin(angles)[:, None, :]
    first_half = values[..., :half_width]
    second = values[..., half_width:]
    return jnp.concatenate(
        [first_half * cosine - second * sine_part, second * cosine + first_half * sine_part], -1
    )


def time_embedding(time_value, embed_width):
    half_width = embed_width // 2
    fraction = jnp.arange(half_width, dtype=jnp.float32) / (half_width - 1)
    period = 0.004 * (4.0 / 0.004) ** fraction
    angles = time_value * (2.0 * jnp.pi) / period
    return jnp.concatenate([jnp.sin(angles), jnp.cos(angles)])


def attend(queries, key_cache, value_cache, action_keys, action_values, is_valid):
    span_rows = queries.shape[0]
    groups = key_cache.shape[1] // HEAD
    group_ratio = queries.shape[1] // key_cache.shape[1]
    query_heads = queries.reshape(span_rows, groups, group_ratio, HEAD)
    prefix_keys = key_cache.reshape(-1, groups, HEAD)
    prefix_values = value_cache.reshape(-1, groups, HEAD)
    own_keys = action_keys.reshape(span_rows, groups, HEAD)
    own_values = action_values.reshape(span_rows, groups, HEAD)
    prefix_scores = jnp.einsum(
        "cgrh,pgh->grcp", query_heads, prefix_keys, preferred_element_type=jnp.float32
    )
    prefix_scores = jnp.where(is_valid[None, None, None, :], prefix_scores, -1e30)
    own_scores = jnp.einsum(
        "cgrh,ngh->grcn", query_heads, own_keys, preferred_element_type=jnp.float32
    )
    row_max = jnp.maximum(jnp.max(prefix_scores, -1), jnp.max(own_scores, -1))[..., None]
    prefix_exp = jnp.exp(prefix_scores - row_max)
    own_exp = jnp.exp(own_scores - row_max)
    prob_total = jnp.sum(prefix_exp, -1, keepdims=True) + jnp.sum(own_exp, -1, keepdims=True)
    prefix_prob = (prefix_exp / prob_total).astype(jnp.bfloat16)
    own_prob = (own_exp / prob_total).astype(jnp.bfloat16)
    attn_mixed = jnp.einsum(
        "grcp,pgh->cgrh", prefix_prob, prefix_values, preferred_element_type=jnp.float32
    )
    attn_mixed = attn_mixed + jnp.einsum(
        "grcn,ngh->cgrh", own_prob, own_values, preferred_element_type=jnp.float32
    )
    return attn_mixed.reshape(span_rows, -1).astype(jnp.bfloat16)


def expert_steps(
    noise_rows,
    length,
    input_weight,
    expert_gain,
    query_w,
    key_w,
    value_w,
    output_w,
    final_gain,
    output_weight,
    key_cache,
    value_cache,
):
    span_rows = noise_rows.shape[0]
    is_valid = jnp.arange(key_cache.shape[0], dtype=jnp.int32) < length
    positions = length.astype(jnp.float32) + jnp.arange(span_rows, dtype=jnp.float32)
    action_state = noise_rows
    for step_idx in range(STEPS):
        time_value = 1.0 - step_idx / STEPS
        hidden = jnp.dot(
            action_state,
            input_weight,
            precision=lax.Precision.HIGHEST,
            preferred_element_type=jnp.float32,
        )
        hidden = hidden + time_embedding(time_value, input_weight.shape[1])[None, :]
        normed = normalize(hidden, expert_gain).astype(jnp.bfloat16)
        raw_queries = jnp.dot(normed, query_w, preferred_element_type=jnp.float32)
        queries = rotate(raw_queries.reshape(span_rows, -1, HEAD), positions).reshape(span_rows, -1)
        queries = (queries * HEAD ** (-0.5)).astype(jnp.bfloat16)
        raw_keys = jnp.dot(normed, key_w, preferred_element_type=jnp.float32)
        action_keys = (
            rotate(raw_keys.reshape(span_rows, -1, HEAD), positions)
            .reshape(span_rows, -1)
            .astype(jnp.bfloat16)
        )
        action_values = jnp.dot(normed, value_w, preferred_element_type=jnp.float32).astype(
            jnp.bfloat16
        )
        attn_mixed = attend(queries, key_cache, value_cache, action_keys, action_values, is_valid)
        hidden = hidden + jnp.dot(attn_mixed, output_w, preferred_element_type=jnp.float32)
        final_normed = normalize(hidden, final_gain).astype(jnp.bfloat16)
        velocity = jnp.dot(final_normed, output_weight, preferred_element_type=jnp.float32)
        action_state = action_state - velocity / STEPS
    return action_state


def shards(
    prefix_hidden,
    prefix_lengths,
    action_noise,
    prefix_gain,
    key_weight,
    value_weight,
    input_weight,
    expert_gain,
    expert_query,
    expert_key,
    expert_value,
    expert_output,
    final_gain,
    output_weight,
):
    gathered = (
        lax.all_gather(expert_query, "wide", axis=0, tiled=True),
        lax.all_gather(expert_key, "wide", axis=0, tiled=True),
        lax.all_gather(expert_value, "wide", axis=0, tiled=True),
        lax.all_gather(expert_output, "wide", axis=0, tiled=True),
    )
    hidden = prefix_hidden[0]
    row_count = hidden.shape[0]
    normed = normalize(hidden.astype(jnp.float32), prefix_gain).astype(jnp.bfloat16)
    stacked = jnp.stack([key_weight, value_weight], 0)
    projected = jnp.einsum(
        "pd,kdc->pkc",
        normed,
        lax.all_gather(stacked, "wide", axis=1, tiled=True),
        preferred_element_type=jnp.float32,
    )
    positions = jnp.arange(row_count, dtype=jnp.float32)
    key_cache = (
        rotate(projected[:, 0].reshape(row_count, -1, HEAD), positions)
        .reshape(row_count, -1)
        .astype(jnp.bfloat16)
    )
    value_cache = projected[:, 1].astype(jnp.bfloat16)
    query_w, key_w, value_w, output_w = gathered
    action_state = expert_steps(
        action_noise[0],
        prefix_lengths[0],
        input_weight,
        expert_gain,
        query_w,
        key_w,
        value_w,
        output_w,
        final_gain,
        output_weight,
        key_cache,
        value_cache,
    )
    return action_state[None]


def solution(mesh):
    placed = (
        P(("groups", "wide"), None, None),
        P(("groups", "wide")),
        P(("groups", "wide"), None, None),
        P(),
        P("wide", None),
        P("wide", None),
        P(),
        P(),
        P("wide", None),
        P("wide", None),
        P("wide", None),
        P("wide", None),
        P(),
        P(),
    )
    return jax.shard_map(
        shards,
        mesh=mesh,
        in_specs=placed,
        out_specs=P(("groups", "wide"), None, None),
        check_vma=False,
    )
```

profile of v0, /device:TPU:0, one launch (start us, length us, event | category | flops | bytes accessed | tf_op | source)
XLA Modules:
  0.0 368.0 jit_solution(7898720133912089493)
XLA Ops:
  8.8 2.3 pad_maximum_fusion
  12.0 3.1 fusion
  19.0 31.2 %all-gather.10.cloned.1.call-done = bf16[1024,512]{1,0:T(8,128)(2,1)} async-done(((bf16[64,512]{1,0:T(8,128)(2,1)}), bf16[1024,512]{1,0:T(8,128)(2,1)}) %all-gather.10.cloned.1.call-update) | async-done | bytes 1048592 | tf_op jit(solution)/shard_map/all_gather | solution.py:135
  50.2 1.5 fusion.107
  51.9 37.4 %all-gather.12.cloned.1.call-done = bf16[1024,512]{1,0:T(8,128)(2,1)} async-done(((bf16[64,512]{1,0:T(8,128)(2,1)}), bf16[1024,512]{1,0:T(8,128)(2,1)}) %all-gather.12.cloned.1.call-update) | async-done | bytes 1048592 | tf_op jit(solution)/shard_map/all_gather | solution.py:136
  89.2 1.5 convolution_convert_fusion.3
  91.4 40.4 %all-gather.8.cloned.1.call-done = bf16[1024,1024]{1,0:T(8,128)(2,1)} async-done(((bf16[64,1024]{1,0:T(8,128)(2,1)}), bf16[1024,1024]{1,0:T(8,128)(2,1)}) %all-gather.8.cloned.1.call-update) | async-done | bytes 2097168 | tf_op jit(solution)/shard_map/all_gather | solution.py:134
  131.9 2.1 fusion.106
  134.6 124.5 %all-gather.6.cloned.1.call-done = bf16[2,8192,512]{2,1,0:T(8,128)(2,1)} async-done(((bf16[2,512,512]{2,1,0:T(8,128)(2,1)}), bf16[2,8192,512]{2,1,0:T(8,128)(2,1)}) %all-gather.6.cloned.1.call-update) | async-done | bytes 16777232 | tf_op jit(solution)/shard_map/all_gather | solution.py:146
  259.1 9.5 %fusion.4 = f32[256,2,512]{2,0,1:T(8,128)S(1)} fusion(bf16[2,8192,512]{2,1,0:T(8,128)(2,1)} %all-gather.6.cloned.1.call-done, bf16[1,256,8192]{2,1,0:T(8,128)(2,1)} %param.14, f32[8192]{0:T(1024)S(1)} %copy-done.58, f32[256]{0:T(256)S(1)} %add_rsqrt_fusion), kind=kOutput, calls=%fused_computation.6 | convolution fusion | flops 4303355904 | bytes 22053888 | tf_op jit(solution)/shard_map/pd,kdc->pkc/dot_general | solution.py:143
  271.2 29.5 %all-gather.14.cloned.1.call-done = bf16[1024,1024]{1,0:T(8,128)(2,1)} async-done(((bf16[64,1024]{1,0:T(8,128)(2,1)}), bf16[1024,1024]{1,0:T(8,128)(2,1)}) %all-gather.14.cloned.1.call-update) | async-done | bytes 2097168 | tf_op jit(solution)/shard_map/all_gather | solution.py:137
  300.8 2.2 multiply_reduce_fusion.6
  306.0 1.7 fusion.100
  307.7 0.9 fusion.109
  308.6 1.6 reshape.311
  310.2 1.1 fusion.96
  311.3 0.8 subtract_convert_fusion.3
  312.1 1.2 fusion.101
  314.1 1.3 fusion.27
  315.5 2.1 fusion.31
  317.6 0.9 convolution_convert_fusion.2
  318.5 1.5 reshape.312
  320.0 1.3 fusion.19
  321.3 0.7 copy.50
  322.0 1.6 convert_element_type.174
  323.6 2.2 multiply_reduce_fusion.4
  329.0 1.1 fusion.102
  330.1 0.9 fusion.111
  331.1 1.6 reshape.314
  332.6 1.1 fusion.95
  333.7 0.8 subtract_convert_fusion.2
  334.5 1.2 fusion.103
  335.7 1.4 fusion.28
  337.2 2.1 fusion.32
  339.3 0.9 convolution_convert_fusion.1
  340.2 1.5 reshape.315
  341.7 1.3 fusion.18
  343.0 0.7 copy.57
  343.7 1.6 convert_element_type.184
  345.3 2.2 multiply_reduce_fusion.2
  347.6 1.0 fusion.23
  348.6 1.2 multiply_reduce_fusion.1
  350.5 0.8 multiply_convert_fusion.1
  354.5 2.3 fusion.33
  356.7 0.9 convolution_convert_fusion
  357.7 0.9 reshape.318
  358.5 1.3 fusion.17
  360.6 0.8 fusion.22
  (221 shorter events, 21.2 us)
Async XLA Ops:
  6.5 9.1 %copy-start = (f32[32,1024]{1,0:T(8,128)S(1)}, f32[32,1024]{1,0:T(8,128)}, u32[]{:S(2)}) copy-start(f32[32,1024]{1,0:T(8,128)} %param.20) | copy-start | bytes 393220
  6.5 43.7 %all-gather.10.cloned.1.call-start = ((), (), s32[]{:S(2)}) async-start(), calls=%async_computation.2 | async-start | bytes 1114112 | tf_op jit(solution)/shard_map/all_gather | solution.py:135
  7.3 82.0 %all-gather.12.cloned.1.call-start = ((), (), s32[]{:S(2)}) async-start(), calls=%async_computation.3 | async-start | bytes 1114112 | tf_op jit(solution)/shard_map/all_gather | solution.py:136
  8.0 123.8 %all-gather.8.cloned.1.call-start = ((), (), s32[]{:S(2)}) async-start(), calls=%async_computation.1 | async-start | bytes 2228224 | tf_op jit(solution)/shard_map/all_gather | solution.py:134
  8.7 250.4 %all-gather.6.cloned.1.call-start = ((), (), s32[]{:S(2)}) async-start(), calls=%async_computation | async-start | bytes 17825792 | tf_op jit(solution)/shard_map/all_gather | solution.py:146
  11.1 289.7 %all-gather.14.cloned.1.call-start = ((), (), s32[]{:S(2)}) async-start(), calls=%async_computation.4 | async-start | bytes 2228224 | tf_op jit(solution)/shard_map/all_gather | solution.py:137
  11.9 3.7 %copy-start.44 = (f32[1,50,32]{1,2,0:T(8,128)S(1)}, f32[1,50,32]{1,2,0:T(8,128)}, u32[]{:S(2)}) copy-start(f32[1,50,32]{1,2,0:T(8,128)} %param.16) | copy-start | bytes 19204
  12.0 6.9 %copy-start.41 = (f32[1024]{0:T(1024)S(1)}, f32[1024]{0:T(1024)}, u32[]{:S(2)}) copy-start(f32[1024]{0:T(1024)} %param.21) | copy-start | bytes 12292
  16.1 117.8 %copy-start.17 = (f32[50,1024]{1,0:T(8,128)}, f32[50,1024]{1,0:T(8,128)S(1)}, u32[]{:S(2)}) copy-start(f32[50,1024]{1,0:T(8,128)S(1)} %get-tuple-element.38) | copy-start | bytes 614404
  17.0 117.0 %copy-start.7 = (f32[50,64]{1,0:T(8,128)}, f32[50,64]{1,0:T(8,128)S(1)}, u32[]{:S(2)}) copy-start(f32[50,64]{1,0:T(8,128)S(1)} %get-tuple-element.33) | copy-start | bytes 38404
  17.0 117.0 %copy-start.12 = (f32[50,64]{1,0:T(8,128)}, f32[50,64]{1,0:T(8,128)S(1)}, u32[]{:S(2)}) copy-start(f32[50,64]{1,0:T(8,128)S(1)} %get-tuple-element.34) | copy-start | bytes 38404
  17.0 252.6 %copy-start.53 = (pred[256]{0:T(512)(128)(4,1)}, pred[256]{0:T(512)(128)(4,1)S(1)}, u32[]{:S(2)}) copy-start(pred[256]{0:T(512)(128)(4,1)S(1)} %iota_compare_fusion) | copy-start | bytes 772
  91.4 167.7 %copy-start.58 = (f32[8192]{0:T(1024)S(1)}, f32[8192]{0:T(1024)}, u32[]{:S(2)}) copy-start(f32[8192]{0:T(1024)} %param.17) | copy-start | bytes 98308
  270.1 30.6 %copy-start.18 = (f32[50,1024]{1,0:T(8,128)S(1)}, f32[50,1024]{1,0:T(8,128)}, u32[]{:S(2)}) copy-start(f32[50,1024]{1,0:T(8,128)} %copy-done.17) | copy-start | bytes 614404
  270.8 32.2 %copy-start.30 = (bf16[1024,32]{0,1:T(8,128)(2,1)S(1)}, bf16[1024,32]{0,1:T(8,128)(2,1)}, u32[]{:S(2)}) copy-start(bf16[1024,32]{0,1:T(8,128)(2,1)} %param.27) | copy-start | bytes 196612
  270.8 32.2 %copy-start.45 = (f32[1,50,32]{1,2,0:T(8,128)S(1)}, f32[1,50,32]{1,2,0:T(8,128)}, u32[]{:S(2)}) copy-start(f32[1,50,32]{1,2,0:T(8,128)} %param.16) | copy-start | bytes 19204
  270.8 32.2 %copy-start.46 = (f32[1024]{0:T(1024)S(1)}, f32[1024]{0:T(1024)}, u32[]{:S(2)}) copy-start(f32[1024]{0:T(1024)} %param.26) | copy-start | bytes 12292
  270.8 32.4 %copy-start.52 = (f32[1024]{0:T(1024)S(1)}, f32[1024]{0:T(1024)}, u32[]{:S(2)}) copy-start(f32[1024]{0:T(1024)} %pad_maximum_fusion.2) | copy-start | bytes 12292
  271.1 32.7 %copy-start.42 = (f32[1024]{0:T(1024)S(1)}, f32[1024]{0:T(1024)}, u32[]{:S(2)}) copy-start(f32[1024]{0:T(1024)} %param.21) | copy-start | bytes 12292
  271.1 33.4 %copy-start.1 = (bf16[1024,1024]{1,0:T(8,128)(2,1)S(1)}, bf16[1024,1024]{1,0:T(8,128)(2,1)}, u32[]{:S(2)}) copy-start(bf16[1024,1024]{1,0:T(8,128)(2,1)} %all-gather.8.cloned.1.call-done) | copy-start | bytes 6291460
  303.2 1.8 copy-start.8
  303.2 1.8 copy-start.13
  304.4 3.2 copy-start.25
  304.9 2.7 copy-start.4
  310.2 7.4 %copy-start.3 = (bf16[1024,512]{1,0:T(8,128)(2,1)S(1)}, bf16[1024,512]{1,0:T(8,128)(2,1)}, u32[]{:S(2)}) copy-start(bf16[1024,512]{1,0:T(8,128)(2,1)} %all-gather.12.cloned.1.call-done) | copy-start | bytes 3145732
  310.2 7.4 %copy-start.26 = (bf16[50,1024]{1,0:T(8,128)(2,1)S(1)}, bf16[50,1024]{1,0:T(8,128)(2,1)}, u32[]{:S(2)}) copy-start(bf16[50,1024]{1,0:T(8,128)(2,1)} %copy-done.25) | copy-start | bytes 307204
  313.3 2.0 copy-start.37
  315.4 2.1 copy-start.57
  323.6 2.3 copy-start.31
  323.6 2.3 copy-start.47
  323.6 2.5 copy-start.51
  323.6 3.7 %copy-start.43 = (f32[1024]{0:T(1024)S(1)}, f32[1024]{0:T(1024)}, u32[]{:S(2)}) copy-start(f32[1024]{0:T(1024)} %param.21) | copy-start | bytes 12292
  326.1 1.9 copy-start.40
  326.2 1.9 copy-start.9
  326.2 1.9 copy-start.14
  327.4 2.7 copy-start.27
  327.9 2.2 copy-start.5
  332.6 6.7 %copy-start.28 = (bf16[50,1024]{1,0:T(8,128)(2,1)S(1)}, bf16[50,1024]{1,0:T(8,128)(2,1)}, u32[]{:S(2)}) copy-start(bf16[50,1024]{1,0:T(8,128)(2,1)} %copy-done.27) | copy-start | bytes 307204
  345.3 2.2 copy-start.32
  348.5 3.3 copy-start.10
  348.5 3.3 copy-start.15
  351.8 1.6 copy-start.11
  351.9 1.6 copy-start.16
  353.3 3.4 copy-start.24
  354.5 5.5 %copy-start.2 = (bf16[1024,1024]{1,0:T(8,128)(2,1)S(1)}, bf16[1024,1024]{1,0:T(8,128)(2,1)}, u32[]{:S(2)}) copy-start(bf16[1024,1024]{1,0:T(8,128)(2,1)} %all-gather.14.cloned.1.call-done) | copy-start | bytes 6291460
  354.5 5.5 %copy-start.20 = (f32[50,1024]{1,0:T(8,128)S(1)}, f32[50,1024]{1,0:T(8,128)}, u32[]{:S(2)}) copy-start(f32[50,1024]{1,0:T(8,128)} %copy-done.19) | copy-start | bytes 614404
  357.6 2.9 copy-start.33
  357.6 2.9 copy-start.48
  (16 other events, 17.1 us)
Sparse Core Ops, SparseCore 0:
  9.5 40.6 all-gather.9
  52.4 36.8 all-gather.11
  91.4 40.4 all-gather.7
  133.9 125.1 all-gather.5
  261.1 39.6 all-gather.13
where the time goes:
time: 369 us; the launch traced here: 368 us
  waiting for transfers between devices  266 us (72%)
  matrix products  50.5 us (14%)
  local copies, waits for them, and re-layouts  20.1 us (5%)
  other arithmetic  16.4 us (4%)
  between operations  15.1 us (4%)
    all_gather x1, waiting for transfers between devices, shards(): lax.all_gather(stacked, 'wide', axis=1, tiled=True)  124 us
    all_gather x1, waiting for transfers between devices, shards(): lax.all_gather(expert_query, 'wide', axis=0, tiled=True)  40.4 us
    all_gather x1, waiting for transfers between devices, shards(): lax.all_gather(expert_value, 'wide', axis=0, tiled=True)  37.4 us
    all_gather x1, waiting for transfers between devices, shards(): lax.all_gather(expert_key, 'wide', axis=0, tiled=True)  31.2 us
    all_gather x1, waiting for transfers between devices, shards(): lax.all_gather(expert_output, 'wide', axis=0, tiled=True)  29.5 us
    dot_general x1, matrix products, shards(): jnp.einsum('pd,kdc->pkc', normed, lax.all_gather(stacked, 'wide', axis=1,...  9.54 us
  transfers between devices with their start and end apart: 5, of which 5 were waited for; matrix products, arithmetic and copies ran while one was open for 7% of the time, Pallas kernels for 0%

commit v1 on v0

--- a/solution.py
+++ b/solution.py
@@ -2,11 +2,28 @@
 import jax.numpy as jnp
 from jax import lax
 from jax.sharding import PartitionSpec as P
+from jax.lax import axis_index, axis_size, ppermute
 
 HEAD = 128
 STEPS = 4
 rope_base = 1000000.0
 norm_eps = 1e-06
+
+
+def turn_terms(x_local, axis_tag):
+    latest, piece_next, z_new = (axis_size(axis_tag), axis_index(axis_tag), x_local.shape[0])
+    current_value, v_now = (x_local, 1)
+    while v_now < latest:
+        views = []
+        u = 0
+        while u < latest:
+            views.append((u, (u - v_now) % latest))
+            u += 1
+        current_value = jnp.concatenate(
+            [current_value, ppermute(current_value, axis_name=axis_tag, perm=views)], 0
+        )
+        v_now = 2 * v_now
+    return jnp.roll(current_value, piece_next * z_new, 0)
 
 
 def normalize(values, norm_gain):
@@ -133,7 +150,7 @@
     gathered = (
         lax.all_gather(expert_query, "wide", axis=0, tiled=True),
         lax.all_gather(expert_key, "wide", axis=0, tiled=True),
-        lax.all_gather(expert_value, "wide", axis=0, tiled=True),
+        turn_terms(expert_value, "wide"),
         lax.all_gather(expert_output, "wide", axis=0, tiled=True),
     )
     hidden = prefix_hidden[0]

time: 369 us -> 347 us (0.940)
  waiting for transfers between devices: 266 us -> 238 us
  starting transfers between devices: 0.16 us -> 8.38 us
    ppermute x0 -> x4, waiting for transfers between devices: none -> 38.6 us  [turn_terms(): ppermute(current_value, axis_name=axis_tag, perm=views)]
    all_gather x1 -> x0, waiting for transfers between devices: 37.4 us -> none  [shards(): lax.all_gather(expert_value, 'wide', axis=0, tiled=True)]
    all_gather x1, waiting for transfers between devices: 31.2 us -> 0.54 us  [shards(): lax.all_gather(expert_key, 'wide', axis=0, tiled=True)]
    ppermute x0 -> x4, starting transfers between devices: none -> 8.26 us  [turn_terms(): ppermute(current_value, axis_name=axis_tag, perm=views)]
  transfers between devices with their start and end apart: 5 -> 8, of which waited for: 5 -> 7; matrix products, arithmetic and copies ran while one was open for 7% -> 8% of each run, Pallas kernels for 0% -> 0%
where the time goes in v1:
time: 347 us; the launch traced here: 346 us
  waiting for transfers between devices  238 us (69%)
  matrix products  48.8 us (14%)
  local copies, waits for them, and re-layouts  18.9 us (5%)
  other arithmetic  17.3 us (5%)
  between operations  15.2 us (4%)
  starting transfers between devices  8.38 us (2%)
    all_gather x1, waiting for transfers between devices, shards(): lax.all_gather(stacked, 'wide', axis=1, tiled=True)  125 us
    all_gather x1, waiting for transfers between devices, shards(): lax.all_gather(expert_query, 'wide', axis=0, tiled=True)  42.8 us
    ppermute x4, waiting for transfers between devices, turn_terms(): ppermute(current_value, axis_name=axis_tag, perm=views)  38.6 us
    all_gather x1, waiting for transfers between devices, shards(): lax.all_gather(expert_output, 'wide', axis=0, tiled=True)  29.6 us
    dot_general x1, matrix products, shards(): jnp.einsum('pd,kdc->pkc', normed, lax.all_gather(stacked, 'wide', axis=1,...  9.54 us
    ppermute x4, starting transfers between devices, turn_terms(): ppermute(current_value, axis_name=axis_tag, perm=views)  8.26 us
    dot_general x4, matrix products, expert_steps(): jnp.dot(attn_mixed, output_w, preferred_element_type=jnp.float32)  7.42 us
  transfers between devices with their start and end apart: 8, of which 7 were waited for; matrix products, arithmetic and copies ran while one was open for 8% of the time, Pallas kernels for 0%

profile of v1, /device:TPU:0, one launch (start us, length us, event | category | flops | bytes accessed | tf_op | source)
XLA Modules:
  0.0 346.2 jit_solution(7345285925508017053)
XLA Ops:
  8.1 2.4 pad_maximum_fusion
  10.5 5.5 %collective-permute-start = (bf16[64,512]{1,0:T(8,128)(2,1)S(1)}, bf16[64,512]{1,0:T(8,128)(2,1)S(1)}, u32[]{:S(2)}, u32[]{:S(2)}) collective-permute-start(bf16[64,512]{1,0:T(8,128)(2,1)S(1)} %copy-done.22), channel_id=1, source_target_pairs={{0,15},{1,0},{2,1},{3,2},{4,3},{5,4},{6,5},{7,6},{8,7},{9,8},{10,9... | collective-permute-start | bytes 196616 | tf_op jit(solution)/shard_map/ppermute | solution.py:23
  16.4 3.1 fusion
  22.6 1.1 collective-permute-start.1
  24.3 3.4 collective-permute-done.1
  28.4 1.3 collective-permute-start.2
  29.7 6.7 %collective-permute-done.2 = bf16[256,512]{1,0:T(8,128)(2,1)S(1)} collective-permute-done((bf16[256,512]{1,0:T(8,128)(2,1)}, bf16[256,512]{1,0:T(8,128)(2,1)S(1)}, u32[]{:S(2)}, u32[]{:S(2)}) %collective-permute-start.2) | collective-permute-done | bytes 262176 | tf_op jit(solution)/shard_map/ppermute | solution.py:23
  37.0 28.6 %collective-permute-done.3 = bf16[512,512]{1,0:T(8,128)(2,1)S(1)} collective-permute-done((bf16[512,512]{1,0:T(8,128)(2,1)S(1)}, bf16[512,512]{1,0:T(8,128)(2,1)S(1)}, u32[]{:S(2)}, u32[]{:S(2)}) %collective-permute-start.3) | collective-permute-done | bytes 524320 | tf_op jit(solution)/shard_map/ppermute | solution.py:23
  66.0 0.9 reshape.309
  67.5 1.5 fusion.115
  69.2 42.8 %all-gather.7.cloned.1.call-done = bf16[1024,1024]{1,0:T(8,128)(2,1)} async-done(((bf16[64,1024]{1,0:T(8,128)(2,1)}), bf16[1024,1024]{1,0:T(8,128)(2,1)}) %all-gather.7.cloned.1.call-update) | async-done | bytes 2097168 | tf_op jit(solution)/shard_map/all_gather | solution.py:151
  112.0 2.1 fusion.114
  114.8 124.6 %all-gather.5.cloned.1.call-done = bf16[2,8192,512]{2,1,0:T(8,128)(2,1)} async-done(((bf16[2,512,512]{2,1,0:T(8,128)(2,1)}), bf16[2,8192,512]{2,1,0:T(8,128)(2,1)}) %all-gather.5.cloned.1.call-update) | async-done | bytes 16777232 | tf_op jit(solution)/shard_map/all_gather | solution.py:163
  239.4 9.5 %fusion.4 = f32[256,2,512]{2,0,1:T(8,128)S(1)} fusion(bf16[2,8192,512]{2,1,0:T(8,128)(2,1)} %all-gather.5.cloned.1.call-done, bf16[1,256,8192]{2,1,0:T(8,128)(2,1)} %param.14, f32[8192]{0:T(1024)S(1)} %copy-done.52, f32[256]{0:T(256)S(1)} %add_rsqrt_fusion), kind=kOutput, calls=%fused_computation.6 | convolution fusion | flops 4303355904 | bytes 22053888 | tf_op jit(solution)/shard_map/pd,kdc->pkc/dot_general | solution.py:160
  251.5 29.6 %all-gather.11.cloned.1.call-done = bf16[1024,1024]{1,0:T(8,128)(2,1)} async-done(((bf16[64,1024]{1,0:T(8,128)(2,1)}), bf16[1024,1024]{1,0:T(8,128)(2,1)}) %all-gather.11.cloned.1.call-update) | async-done | bytes 2097168 | tf_op jit(solution)/shard_map/all_gather | solution.py:154
  281.1 2.2 multiply_reduce_fusion.6
  284.2 2.2 convolution_convert_fusion.2
  287.9 1.7 fusion.108
  289.5 0.9 fusion.117
  290.5 1.6 reshape.311
  292.1 1.1 fusion.104
  293.1 0.8 subtract_convert_fusion.3
  293.9 1.2 fusion.109
  295.9 1.3 fusion.31
  297.8 2.1 fusion.35
  299.9 1.4 reshape.312
  301.4 1.3 fusion.19
  303.4 1.6 convert_element_type.174
  305.0 2.3 multiply_reduce_fusion.4
  309.0 0.9 convolution_convert_fusion.1
  311.5 1.1 fusion.110
  312.5 0.9 fusion.119
  313.5 1.6 reshape.314
  315.0 1.1 fusion.103
  316.1 0.8 subtract_convert_fusion.2
  316.9 1.2 fusion.111
  318.2 1.4 fusion.32
  319.6 2.1 fusion.36
  321.7 1.4 reshape.315
  323.1 1.3 fusion.18
  325.2 1.6 convert_element_type.184
  326.8 2.3 multiply_reduce_fusion.2
  329.1 1.0 fusion.23
  330.1 1.2 multiply_reduce_fusion.1
  332.0 0.8 multiply_convert_fusion.1
  332.8 0.9 convolution_convert_fusion
  336.3 1.5 fusion.37
  338.8 0.8 fusion.22
  (227 shorter events, 22.5 us)
Async XLA Ops:
  6.5 13.5 %copy-start = (f32[32,1024]{1,0:T(8,128)S(1)}, f32[32,1024]{1,0:T(8,128)}, u32[]{:S(2)}) copy-start(f32[32,1024]{1,0:T(8,128)} %param.20) | copy-start | bytes 393220
  6.5 4.0 %copy-start.22 = (bf16[64,512]{1,0:T(8,128)(2,1)S(1)}, bf16[64,512]{1,0:T(8,128)(2,1)}, u32[]{:S(2)}) copy-start(bf16[64,512]{1,0:T(8,128)(2,1)} %param.24) | copy-start | bytes 196612
  6.5 60.9 %all-gather.9.cloned.1.call-start = ((), (), s32[]{:S(2)}) async-start(), calls=%async_computation.2 | async-start | bytes 1114112 | tf_op jit(solution)/shard_map/all_gather | solution.py:152
  7.3 104.7 %all-gather.7.cloned.1.call-start = ((), (), s32[]{:S(2)}) async-start(), calls=%async_computation.1 | async-start | bytes 2228224 | tf_op jit(solution)/shard_map/all_gather | solution.py:151
  8.0 231.4 %all-gather.5.cloned.1.call-start = ((), (), s32[]{:S(2)}) async-start(), calls=%async_computation | async-start | bytes 17825792 | tf_op jit(solution)/shard_map/all_gather | solution.py:163
  10.5 270.6 %all-gather.11.cloned.1.call-start = ((), (), s32[]{:S(2)}) async-start(), calls=%async_computation.3 | async-start | bytes 2228224 | tf_op jit(solution)/shard_map/all_gather | solution.py:154
  10.5 12.1 %collective-permute-start = (bf16[64,512]{1,0:T(8,128)(2,1)S(1)}, bf16[64,512]{1,0:T(8,128)(2,1)S(1)}, u32[]{:S(2)}, u32[]{:S(2)}) collective-permute-start(bf16[64,512]{1,0:T(8,128)(2,1)S(1)} %copy-done.22), channel_id=1, source_target_pairs={{0,15},{1,0},{2,1},{3,2},{4,3},{5,4},{6,5},{7,6},{8,7},{9,8},{10,9... | collective-permute-start | bytes 196616 | tf_op jit(solution)/shard_map/ppermute | solution.py:23
  16.3 3.7 %copy-start.38 = (f32[1,50,32]{1,2,0:T(8,128)S(1)}, f32[1,50,32]{1,2,0:T(8,128)}, u32[]{:S(2)}) copy-start(f32[1,50,32]{1,2,0:T(8,128)} %param.16) | copy-start | bytes 19204
  16.4 13.3 %copy-start.35 = (f32[1024]{0:T(1024)S(1)}, f32[1024]{0:T(1024)}, u32[]{:S(2)}) copy-start(f32[1024]{0:T(1024)} %param.21) | copy-start | bytes 12292
  21.4 92.8 %copy-start.7 = (f32[50,64]{1,0:T(8,128)}, f32[50,64]{1,0:T(8,128)S(1)}, u32[]{:S(2)}) copy-start(f32[50,64]{1,0:T(8,128)S(1)} %get-tuple-element.33) | copy-start | bytes 38404
  21.4 92.8 %copy-start.12 = (f32[50,64]{1,0:T(8,128)}, f32[50,64]{1,0:T(8,128)S(1)}, u32[]{:S(2)}) copy-start(f32[50,64]{1,0:T(8,128)S(1)} %get-tuple-element.34) | copy-start | bytes 38404
  22.6 5.0 %collective-permute-start.1 = (bf16[128,512]{1,0:T(8,128)(2,1)S(1)}, bf16[128,512]{1,0:T(8,128)(2,1)S(1)}, u32[]{:S(2)}, u32[]{:S(2)}) collective-permute-start(bf16[128,512]{1,0:T(8,128)(2,1)S(1)} %pad_maximum_fusion.3), channel_id=1, source_target_pairs={{0,14},{1,15},{2,0},{3,1},{4,2},{5,3},{6,4},{7,5},{8,6},{9,7},{10,... | collective-permute-start | bytes 393224 | tf_op jit(solution)/shard_map/ppermute | solution.py:23
  28.4 8.1 %collective-permute-start.2 = (bf16[256,512]{1,0:T(8,128)(2,1)}, bf16[256,512]{1,0:T(8,128)(2,1)S(1)}, u32[]{:S(2)}, u32[]{:S(2)}) collective-permute-start(bf16[256,512]{1,0:T(8,128)(2,1)} %pad_maximum_fusion.2), channel_id=1, source_target_pairs={{0,12},{1,13},{2,14},{3,15},{4,0},{5,1},{6,2},{7,3},{8,4},{9,5},{1... | collective-permute-start | bytes 786440 | tf_op jit(solution)/shard_map/ppermute | solution.py:23
  29.6 220.3 %copy-start.47 = (pred[256]{0:T(512)(128)(4,1)}, pred[256]{0:T(512)(128)(4,1)S(1)}, u32[]{:S(2)}) copy-start(pred[256]{0:T(512)(128)(4,1)S(1)} %iota_compare_fusion) | copy-start | bytes 772
  36.5 29.1 %collective-permute-start.3 = (bf16[512,512]{1,0:T(8,128)(2,1)S(1)}, bf16[512,512]{1,0:T(8,128)(2,1)S(1)}, u32[]{:S(2)}, u32[]{:S(2)}) collective-permute-start(bf16[512,512]{1,0:T(8,128)(2,1)S(1)} %pad_maximum_fusion.1), channel_id=1, source_target_pairs={{0,8},{1,9},{2,10},{3,11},{4,12},{5,13},{6,14},{7,15},{8,0},{9,1},... | collective-permute-start | bytes 1572872 | tf_op jit(solution)/shard_map/ppermute | solution.py:23
  65.7 48.4 %copy-start.4 = (bf16[2048,512]{1,0:T(8,128)(2,1)}, bf16[2048,512]{1,0:T(8,128)(2,1)S(1)}, u32[]{:S(2)}) copy-start(bf16[2048,512]{1,0:T(8,128)(2,1)S(1)} %constant_dynamic-update-slice_fusion) | copy-start | bytes 6291460
  69.2 170.2 %copy-start.52 = (f32[8192]{0:T(1024)S(1)}, f32[8192]{0:T(1024)}, u32[]{:S(2)}) copy-start(f32[8192]{0:T(1024)} %param.17) | copy-start | bytes 98308
  249.3 1.4 copy-start.31
  251.0 32.2 %copy-start.23 = (bf16[1024,32]{0,1:T(8,128)(2,1)S(1)}, bf16[1024,32]{0,1:T(8,128)(2,1)}, u32[]{:S(2)}) copy-start(bf16[1024,32]{0,1:T(8,128)(2,1)} %param.27) | copy-start | bytes 196612
  251.1 32.2 %copy-start.39 = (f32[1,50,32]{1,2,0:T(8,128)S(1)}, f32[1,50,32]{1,2,0:T(8,128)}, u32[]{:S(2)}) copy-start(f32[1,50,32]{1,2,0:T(8,128)} %param.16) | copy-start | bytes 19204
  251.1 32.2 %copy-start.40 = (f32[1024]{0:T(1024)S(1)}, f32[1024]{0:T(1024)}, u32[]{:S(2)}) copy-start(f32[1024]{0:T(1024)} %param.26) | copy-start | bytes 12292
  251.1 32.4 %copy-start.46 = (f32[1024]{0:T(1024)S(1)}, f32[1024]{0:T(1024)}, u32[]{:S(2)}) copy-start(f32[1024]{0:T(1024)} %pad_maximum_fusion.5) | copy-start | bytes 12292
  251.3 32.7 %copy-start.36 = (f32[1024]{0:T(1024)S(1)}, f32[1024]{0:T(1024)}, u32[]{:S(2)}) copy-start(f32[1024]{0:T(1024)} %param.21) | copy-start | bytes 12292
  251.5 34.8 %copy-start.1 = (bf16[1024,1024]{1,0:T(8,128)(2,1)S(1)}, bf16[1024,1024]{1,0:T(8,128)(2,1)}, u32[]{:S(2)}) copy-start(bf16[1024,1024]{1,0:T(8,128)(2,1)} %all-gather.7.cloned.1.call-done) | copy-start | bytes 6291460
  284.0 2.3 copy-start.19
  284.2 2.7 copy-start.8
  284.2 2.7 copy-start.13
  286.3 1.5 copy-start.48
  286.8 2.7 copy-start.3
  295.1 2.0 copy-start.29
  295.9 1.4 copy-start.44
  305.0 2.4 copy-start.24
  305.0 2.4 copy-start.41
  305.0 2.6 copy-start.45
  305.0 3.9 %copy-start.37 = (f32[1024]{0:T(1024)S(1)}, f32[1024]{0:T(1024)}, u32[]{:S(2)}) copy-start(f32[1024]{0:T(1024)} %param.21) | copy-start | bytes 12292
  305.0 3.9 %copy-start.5 = (bf16[2048,512]{1,0:T(8,128)(2,1)S(1)}, bf16[2048,512]{1,0:T(8,128)(2,1)}, u32[]{:S(2)}) copy-start(bf16[2048,512]{1,0:T(8,128)(2,1)} %copy-done.4) | copy-start | bytes 6291460
  309.0 1.5 copy-start.9
  309.0 1.5 copy-start.14
  309.9 1.5 copy-start.49
  318.1 1.4 copy-start.30
  326.8 2.4 copy-start.25
  326.8 6.0 %copy-start.6 = (bf16[2048,512]{1,0:T(8,128)(2,1)S(1)}, bf16[2048,512]{1,0:T(8,128)(2,1)}, u32[]{:S(2)}) copy-start(bf16[2048,512]{1,0:T(8,128)(2,1)} %copy-done.4) | copy-start | bytes 6291460
  332.8 1.5 copy-start.10
  332.8 1.5 copy-start.15
  334.3 1.2 copy-start.11
  335.4 2.4 copy-start.33
  336.2 2.0 copy-start.2
  336.2 2.0 copy-start.18
  (13 other events, 11.3 us)
Sparse Core Ops, SparseCore 0:
  9.5 57.9 all-gather.8
  69.6 42.3 all-gather.6
  114.2 125.1 all-gather.4
  241.4 39.6 all-gather.10
